TPU v7x, 32 devices: a whole 2x2x4 slice. The times are simulated.
32 devices in a mesh: row: 4 (over y, x), col: 8 (over z, core).
Axes of the slice: x: 2, y: 2, z: 4, core: 2. Of those that a mesh axis runs over, the one named last changes fastest.
Arguments:
- matrix: float32 [6, 4, 128, 128, 8, 128], P(None, 'row', None, None, 'col'), may hold values from -6 to 6
- factors: float32 [10, 512, 512], P(None, None, 'col'), as said below
- starts: int32 [10], replicated, may hold values from 0 to 2560, as said below
Outputs:
- updated: float32 [6, 4, 128, 128, 8, 128], P(None, 'row', None, None, 'col')
Inputs may be any that keep to these rules, and one draw needn't show every extreme that they name: starts[w] = starts[0] + 256 * w, and starts[0] is a multiple of 128. Each factors[w] is orthogonal.
All inputs are finite; a program needn't handle non-finite values.
Results may differ from a plain program's by a relative error of at most 0.0001.
Values sent between devices are 32-bit elements; how exact they have to be, the bound alone decides.
No kernel may reach another device: no remote copies, remote signals or barrier semaphores. Data moves between devices by JAX's collectives and lax.ppermute only.
A program may use at most 384 MiB of HBM per device.

v0:
```python
import jax
import jax.numpy as jnp
from jax import lax
from jax.sharding import PartitionSpec as P

WIN = 512
SHIFT = 256
WINS = 10


def pick_tiles(first_tile, per_device, axis_count, position, span_tiles):
    global_tiles = (
        first_tile
        + jnp.remainder(position - first_tile, axis_count)
        + jnp.arange(per_device, dtype=jnp.int32) * axis_count
    )
    tile_valid = global_tiles < first_tile + span_tiles
    return (tile_valid, jnp.where(tile_valid, global_tiles // axis_count, 0))


def band_order(first_tile, axis_count, per_device, span_tiles):
    places = jnp.arange(span_tiles, dtype=jnp.int32)
    return jnp.remainder(first_tile + places, axis_count) * per_device + places // axis_count


def slot_order(first_tile, axis_count, per_device, span_tiles):
    slot_ids = jnp.arange(axis_count * per_device, dtype=jnp.int32)
    places = (
        jnp.remainder(slot_ids // per_device - first_tile, axis_count)
        + slot_ids % per_device * axis_count
    )
    slot_valid = places < span_tiles
    return (slot_valid, jnp.where(slot_valid, places, 0))


def body(matrix, factors, starts):
    row_count = lax.axis_size("row")
    col_count = lax.axis_size("col")
    row_place = lax.axis_index("row")
    col_place = lax.axis_index("col")
    row_cycles = matrix.shape[0]
    tile_size = matrix.shape[2]
    col_cycles = matrix.shape[3]
    span_tiles = (WIN + SHIFT * (WINS - 1)) // tile_size
    first_tile = starts[0] // tile_size
    all_factors = lax.all_gather(factors, "col", axis=2, tiled=True)

    def left_step(window, band_rows):
        offset_row = starts[window] - starts[0]
        factor_now = lax.dynamic_index_in_dim(all_factors, window, 0, keepdims=False)
        window_rows = lax.dynamic_slice_in_dim(band_rows, offset_row, WIN, 0)
        result_rows = jnp.dot(
            factor_now.T,
            window_rows,
            precision=lax.Precision.HIGHEST,
            preferred_element_type=jnp.float32,
        )
        return lax.dynamic_update_slice_in_dim(band_rows, result_rows, offset_row, 0)

    def right_step(window, band_cols):
        offset_col = starts[window] - starts[0]
        factor_now = lax.dynamic_index_in_dim(all_factors, window, 0, keepdims=False)
        window_cols = lax.dynamic_slice_in_dim(band_cols, offset_col, WIN, 1)
        result_cols = jnp.dot(
            window_cols,
            factor_now,
            precision=lax.Precision.HIGHEST,
            preferred_element_type=jnp.float32,
        )
        return lax.dynamic_update_slice_in_dim(band_cols, result_cols, offset_col, 1)

    local_tiles = matrix.reshape(row_cycles, tile_size, col_cycles * tile_size)
    rows_each = -(-span_tiles // row_count)
    row_valid, row_index = pick_tiles(first_tile, rows_each, row_count, row_place, span_tiles)
    picked = jnp.where(row_valid[:, None, None], jnp.take(local_tiles, row_index, axis=0), 0.0)
    received = lax.all_to_all(picked, "row", split_axis=2, concat_axis=0, tiled=True)
    band_rows = jnp.take(received, band_order(first_tile, row_count, rows_each, span_tiles), axis=0)
    band_rows = band_rows.reshape(span_tiles * tile_size, received.shape[2])
    band_rows = lax.fori_loop(0, WINS, left_step, band_rows)
    row_tiles = band_rows.reshape(span_tiles, tile_size, received.shape[2])
    send_valid, send_place = slot_order(first_tile, row_count, rows_each, span_tiles)
    backsend = jnp.where(send_valid[:, None, None], jnp.take(row_tiles, send_place, axis=0), 0.0)
    returned = lax.all_to_all(backsend, "row", split_axis=0, concat_axis=2, tiled=True)
    for member in range(rows_each):
        local_tiles = jnp.where(
            row_valid[member],
            lax.dynamic_update_index_in_dim(local_tiles, returned[member], row_index[member], 0),
            local_tiles,
        )
    local_rows = row_cycles * tile_size
    column_view = local_tiles.reshape(local_rows, col_cycles, tile_size)
    cols_each = -(-span_tiles // col_count)
    col_valid, col_index = pick_tiles(first_tile, cols_each, col_count, col_place, span_tiles)
    picked_cols = jnp.where(col_valid[None, :, None], jnp.take(column_view, col_index, axis=1), 0.0)
    col_order = band_order(first_tile, col_count, cols_each, span_tiles)
    received_cols = lax.all_to_all(picked_cols, "col", split_axis=0, concat_axis=1, tiled=True)
    share_rows = received_cols.shape[0]
    band_cols = jnp.take(received_cols, col_order, axis=1).reshape(
        share_rows, span_tiles * tile_size
    )
    band_cols = lax.fori_loop(0, WINS, right_step, band_cols)
    slot_valid, slot_place = slot_order(first_tile, col_count, cols_each, span_tiles)
    send_cols = jnp.where(
        slot_valid[None, :, None],
        jnp.take(band_cols.reshape(share_rows, span_tiles, tile_size), slot_place, axis=1),
        0.0,
    )
    returned_cols = lax.all_to_all(send_cols, "col", split_axis=1, concat_axis=0, tiled=True)
    for member in range(cols_each):
        column_view = jnp.where(
            col_valid[member],
            lax.dynamic_update_index_in_dim(
                column_view, returned_cols[:, member], col_index[member], 1
            ),
            column_view,
        )
    return column_view.reshape(matrix.shape)


def solution(mesh):
    placed = (P(None, "row", None, None, "col", None), P(None, None, "col"), P())
    return jax.shard_map(
        body,
        mesh=mesh,
        in_specs=placed,
        out_specs=P(None, "row", None, None, "col", None),
        check_vma=False,
    )
```

profile of v0, /device:TPU:2, one launch (start us, length us, event | category | flops | bytes accessed | tf_op | source)
XLA Modules:
  0.0 2669.3 jit_solution(13656926926000482717)
XLA Ops:
  9.7 133.3 %reduce.3 = f32[6,128,128,128]{3,2,1,0:T(8,128)} reduce(f32[6,1,128,128,1,128]{5,4,3,2,1,0:T(1,128)} %param.7, f32[]{:T(128)} %broadcast.1276), dimensions={1,4}, to_apply=%param.7.reduce_sub_computation.3 | reduce | bytes 100663296 | tf_op args[0]
  143.0 53.6 %reshape.633 = f32[6,128,16384]{2,1,0:T(8,128)} reshape(f32[6,128,128,128]{3,2,1,0:T(8,128)} %reduce.3) | data formatting | bytes 100663296 | tf_op jit(solution)/shard_map/reshape | solution.py:72
  196.6 22.3 fusion.49
  273.7 34.3 %fusion.10 = f32[6,128,16384]{2,1,0:T(8,128)} fusion(f32[6,128,5376]{2,1,0:T(8,128)} %gather_fusion.7, f32[6,128,5504]{2,1,0:T(8,128)} %gather_fusion.6, f32[6,128,5504]{2,1,0:T(8,128)} %gather_fusion.5, pred[6]{0:T(512)(128)(4,1)S(1)} %get-tuple-element.199, pred[6]{0:T(512)(128)(4,1)S(1)} %get-tuple-element.236), kind=kLoop, calls=%fused_computation.19 | loop fusion | flops 50331648 | bytes 100663312 | tf_op jit(solution)/shard_map/jit(_where)/select_n | solution.py:75
  308.0 58.4 %copy.74 = f32[6,128,16384]{1,0,2:T(8,128)} copy(f32[6,128,16384]{2,1,0:T(8,128)} %fusion.10) | data formatting | bytes 100663296 | tf_op jit(solution)/shard_map/jit(_where)/select_n | solution.py:75
  380.9 102.0 %all-gather.2.cloned.1.call-done = f32[10,512,512]{1,2,0:T(8,128)} async-done(((f32[10,512,64]{1,2,0:T(8,128)}), f32[10,512,512]{1,2,0:T(8,128)}) %all-gather.2.cloned.1.call-update) | async-done | bytes 10485776 | tf_op jit(solution)/shard_map/all_gather | solution.py:46
  494.1 606.8 %all-to-all-done = f32[6,128,16384]{1,0,2:T(8,128)} async-done(((f32[6,128,16384]{1,0,2:T(8,128)}), f32[6,128,16384]{1,0,2:T(8,128)}, u32[]{:S(2)}, u32[]{:S(2)}) %all-to-all-start) | async-done | bytes 50331680 | tf_op jit(solution)/shard_map/all_to_all | solution.py:76
  1100.9 58.1 %copy.76 = f32[4,6,128,4096]{3,2,1,0:T(8,128)} copy(f32[4,6,128,4096]{2,1,3,0:T(8,128)} %bitcast.10) | data formatting | bytes 100663296 | tf_op jit(solution)/shard_map/all_to_all | solution.py:76
  1159.1 32.2 %gather_fusion = f32[22,128,4096]{2,1,0:T(8,128)} fusion(f32[24,128,4096]{2,1,0:T(8,128)} %bitcast.115, s32[1024]{0:T(1024)S(1)} %pad_clamp_fusion.4), kind=kCustom, calls=%fused_computation | custom fusion | bytes 92274776 | tf_op jit(solution)/shard_map/jit(_take)/gather | solution.py:77
  1191.3 34.3 %bitcast_select_fusion = f32[2816,4096]{1,0:T(8,128)} fusion(f32[22,128,4096]{2,1,0:T(8,128)} %gather_fusion, pred[2816]{0:T(1024)(128)(4,1)S(1)} %broadcast_bitcast_fusion.1), kind=kLoop, calls=%fused_computation.21 | loop fusion | flops 11534336 | bytes 92277504 | tf_op jit(solution)/shard_map/jit(_take)/select_n | solution.py:77
  1225.5 415.1 %while.26 = (s32[]{:T(128)}, f32[2816,4096]{1,0:T(8,128)}, f32[10,512,512]{2,1,0:T(8,128)}, s32[10]{0:T(128)S(1)}, s32[]{:T(128)}, /*index=5*/s32[]{:T(128)}, s32[]{:T(128)}) while((s32[]{:T(128)}, f32[2816,4096]{1,0:T(8,128)}, f32[10,512,512]{2,1,0:T(8,128)}, s32[10]{0:T(128)S(1)}, s32[]{:T(128)}, /*index=5*/s32[]{:T(128)}, s32[]{:T(128)}) %tuple.96), condition=%wide.region_1.2_spmd, body=%wide.region_0.1_spmd.sunk | while | flops 12884901888 | bytes 34603672 | solution.py:79
  1244.8 22.3 dynamic_update_slice.27
  1286.4 22.3 dynamic_update_slice.27
  1328.0 22.2 dynamic_update_slice.27
  1369.5 22.3 dynamic_update_slice.27
  1393.7 17.4 fusion.67
  1411.1 22.2 dynamic_update_slice.27
  1452.7 22.3 dynamic_update_slice.27
  1494.3 22.2 dynamic_update_slice.27
  1518.5 17.4 fusion.67
  1535.9 22.3 dynamic_update_slice.27
  1577.5 22.2 dynamic_update_slice.27
  1619.0 21.7 dynamic_update_slice.27
  1640.7 35.0 %gather_fusion.1 = f32[24,128,4096]{2,1,0:T(8,128)} fusion(f32[22,128,4096]{2,1,0:T(8,128)} %bitcast.111, s32[1024]{0:T(1024)S(1)} %pad_clamp_fusion.3), kind=kCustom, calls=%fused_computation.1 | custom fusion | bytes 100663392 | tf_op jit(solution)/shard_map/jit(_take)/gather | solution.py:82
  1675.7 35.7 %select_select_fusion = f32[24,128,4096]{2,1,0:T(8,128)} fusion(f32[24,128,4096]{2,1,0:T(8,128)} %gather_fusion.1, pred[24]{0:T(512)(128)(4,1)S(1)} %copy-done.8, pred[24]{0:T(512)(128)(4,1)S(1)} %copy-done.9), kind=kLoop, calls=%fused_computation.20 | loop fusion | flops 25165824 | bytes 100663344 | tf_op jit(solution)/shard_map/jit(_where)/select_n | solution.py:82
  1738.0 527.0 %all-to-all-done.1 = f32[24,128,4096]{2,1,0:T(8,128)} async-done(((f32[24,128,4096]{2,1,0:T(8,128)}), f32[24,128,4096]{2,1,0:T(8,128)}, u32[]{:S(2)}, u32[]{:S(2)}) %all-to-all-start.1) | async-done | bytes 50331680 | tf_op jit(solution)/shard_map/all_to_all | solution.py:83
  2265.0 33.1 %slice_bitcast_fusion = (f32[4,1,16,8,4096]{4,3,2,1,0:T(8,128)}, f32[4,1,16,8,4096]{4,3,2,1,0:T(8,128)}, f32[4,1,16,8,4096]{4,3,2,1,0:T(8,128)}, f32[4,1,16,8,40...) fusion(f32[6,128,4,4096]{3,1,0,2:T(8,128)} %bitcast.17), kind=kLoop, calls=%fused_computation.22 | loop fusion | bytes 100663296
  2395.8 41.2 %copy.102 = f32[96,8,128,128]{3,2,1,0:T(8,128)} copy(f32[96,8,128,128]{3,1,2,0:T(8,128)} %bitcast.110) | data formatting | bytes 100663296
  2437.1 46.1 %copy.84 = f32[768,128,128]{2,0,1:T(8,128)} copy(f32[768,128,128]{2,1,0:T(8,128)} %bitcast.112) | data formatting | bytes 100663296 | tf_op jit(solution)/shard_map/reshape | solution.py:91
  2492.5 37.6 %all-to-all-done.2 = f32[768,3,128]{2,1,0:T(4,128)S(1)} async-done(((f32[768,3,128]{2,1,0:T(4,128)}), f32[768,3,128]{2,1,0:T(4,128)S(1)}, u32[]{:S(2)}, u32[]{:S(2)}) %all-to-all-start.2) | async-done | bytes 1179680 | tf_op jit(solution)/shard_map/all_to_all | solution.py:96
  2531.1 52.1 %while.27 = (s32[]{:T(128)}, f32[96,2816]{1,0:T(8,128)S(1)}, s32[10]{0:T(128)S(1)}, f32[10,512,512]{2,1,0:T(8,128)}, s32[]{:T(128)}, /*index=5*/s32[]{:T(128)}, s32[]{:T(128)}) while((s32[]{:T(128)}, f32[96,2816]{1,0:T(8,128)S(1)}, s32[10]{0:T(128)S(1)}, f32[10,512,512]{2,1,0:T(8,128)}, s32[]{:T(128)}, /*index=5*/s32[]{:T(128)}, ...), condition=%wide.region_3.4_spmd, body=%wide.region_2.3_spmd.sunk | while | flops 301989888 | bytes 1835671 | solution.py:101
  2595.4 22.6 all-to-all-done.3
  (158 shorter events, 440.9 us)
Async XLA Ops:
  230.7 43.1 %copy-start.2 = (pred[6]{0:T(512)(128)(4,1)}, pred[6]{0:T(512)(128)(4,1)S(1)}, u32[]{:S(2)}) copy-start(pred[6]{0:T(512)(128)(4,1)S(1)} %get-tuple-element.236) | copy-start | bytes 22
  366.4 734.6 %all-to-all-start = ((f32[6,128,16384]{1,0,2:T(8,128)}), f32[6,128,16384]{1,0,2:T(8,128)}, u32[]{:S(2)}, u32[]{:S(2)}) async-start(f32[6,128,16384]{1,0,2:T(8,128)} %copy.74), calls=%async_computation | async-start | bytes 134217728 | tf_op jit(solution)/shard_map/all_to_all | solution.py:76
  379.4 103.5 %all-gather.2.cloned.1.call-start = ((), (), s32[]{:S(2)}) async-start(), calls=%async_computation.4 | async-start | bytes 11796480 | tf_op jit(solution)/shard_map/all_gather | solution.py:46
  1191.3 34.3 %copy-start = (s32[10]{0:T(128)S(1)}, s32[10]{0:T(128)}, u32[]{:S(2)}) copy-start(s32[10]{0:T(128)} %param.9) | copy-start | bytes 124
  1640.7 35.0 %copy-start.8 = (pred[24]{0:T(512)(128)(4,1)S(1)}, pred[24]{0:T(512)(128)(4,1)}, u32[]{:S(2)}) copy-start(pred[24]{0:T(512)(128)(4,1)} %get-tuple-element.233) | copy-start | bytes 76
  1640.7 35.0 %copy-start.9 = (pred[24]{0:T(512)(128)(4,1)S(1)}, pred[24]{0:T(512)(128)(4,1)}, u32[]{:S(2)}) copy-start(pred[24]{0:T(512)(128)(4,1)} %get-tuple-element.234) | copy-start | bytes 76
  1711.4 12.7 copy-start.4
  1711.4 25.9 copy-start.3
  1711.4 553.6 %all-to-all-start.1 = ((f32[24,128,4096]{2,1,0:T(8,128)}), f32[24,128,4096]{2,1,0:T(8,128)}, u32[]{:S(2)}, u32[]{:S(2)}) async-start(f32[24,128,4096]{2,1,0:T(8,128)} %select_select_fusion), calls=%async_computation.1 | async-start | bytes 100663296 | tf_op jit(solution)/shard_map/all_to_all | solution.py:83
  2298.1 7.8 slice-start.8
  2298.1 7.8 slice-start.9
  2305.9 4.8 slice-start.6
  2305.9 6.5 slice-start.7
  2310.7 6.0 slice-start.4
  2312.4 4.6 slice-start.5
  2316.7 5.1 slice-start.2
  2317.1 6.2 slice-start.3
  2321.9 5.6 slice-start
  2323.2 4.5 slice-start.1
  2437.0 48.2 %copy-start.5 = (pred[3]{0:T(512)(128)(4,1)S(1)}, pred[3]{0:T(512)(128)(4,1)}, u32[]{:S(2)}) copy-start(pred[3]{0:T(512)(128)(4,1)} %get-tuple-element.235) | copy-start | bytes 13
  2437.0 48.2 %copy-start.7 = (pred[3]{0:T(512)(128)(4,1)S(1)}, pred[3]{0:T(512)(128)(4,1)}, u32[]{:S(2)}) copy-start(pred[3]{0:T(512)(128)(4,1)} %get-tuple-element.197) | copy-start | bytes 13
  2483.2 47.9 %copy-start.1 = (s32[10]{0:T(128)S(1)}, s32[10]{0:T(128)}, u32[]{:S(2)}) copy-start(s32[10]{0:T(128)} %param.9) | copy-start | bytes 124
  2487.5 42.7 %all-to-all-start.2 = ((f32[768,3,128]{2,1,0:T(4,128)}), f32[768,3,128]{2,1,0:T(4,128)S(1)}, u32[]{:S(2)}, u32[]{:S(2)}) async-start(f32[768,3,128]{2,1,0:T(4,128)} %copy.85), calls=%async_computation.2 | async-start | bytes 3145728 | tf_op jit(solution)/shard_map/all_to_all | solution.py:96
  2531.0 57.8 %copy-start.6 = (s32[3]{0:T(128)S(1)}, s32[3]{0:T(128)}, u32[]{:S(2)}) copy-start(s32[3]{0:T(128)} %get-tuple-element.198) | copy-start | bytes 40
  2585.2 32.9 %all-to-all-start.3 = ((f32[96,24,128]{2,0,1:T(8,128)}), f32[96,24,128]{2,0,1:T(8,128)S(1)}, u32[]{:S(2)}, u32[]{:S(2)}) async-start(f32[96,24,128]{2,0,1:T(8,128)} %select_bitcast_fusion), calls=%async_computation.3 | async-start | bytes 2359296 | tf_op jit(solution)/shard_map/all_to_all | solution.py:108
Sparse Core Ops, SparseCore 0:
  381.8 101.0 all-gather.1
where the time goes:
time: 2690 us; the launch traced here: 2670 us
  waiting for transfers between devices  1300 us (48%)
  local copies, waits for them, and re-layouts  772 us (29%)
  other arithmetic  315 us (12%)
  matrix products  194 us (7%)
  starting transfers between devices  34.7 us (1%)
  between operations  33.2 us (1%)
    all_to_all x1, waiting for transfers between devices, body(): lax.all_to_all(picked, 'row', split_axis=2, concat_axis=0, tiled=True)  607 us
    all_to_all x1, waiting for transfers between devices, body(): lax.all_to_all(backsend, 'row', split_axis=0, concat_axis=2, tiled=True)  527 us
    dynamic_update_slice x10, local copies, waits for them, and re-layouts, left_step(): lax.dynamic_update_slice_in_dim(band_rows, result_rows, offset_row, 0)  222 us
    dot_general x10, matrix products, left_step(): jnp.dot(factor_now.T, window_rows, precision=lax.Precision.HIGHEST, prefe...  174 us
    unnamed x6, other arithmetic  133 us
    all_gather x1, waiting for transfers between devices, body(): all_factors = lax.all_gather(factors, 'col', axis=2, tiled=True)  102 us
    unnamed x43, local copies, waits for them, and re-layouts  78.5 us
    gather x5, local copies, waits for them, and re-layouts, body(): jnp.take(local_tiles, row_index, axis=0)  76.6 us
  transfers between devices with their start and end apart: 5, of which 5 were waited for; matrix products, arithmetic and copies ran while one was open for 1% of the time, Pallas kernels for 0%

commit v1 on v0

--- a/solution.py
+++ b/solution.py
@@ -73,7 +73,9 @@
     rows_each = -(-span_tiles // row_count)
     row_valid, row_index = pick_tiles(first_tile, rows_each, row_count, row_place, span_tiles)
     picked = jnp.where(row_valid[:, None, None], jnp.take(local_tiles, row_index, axis=0), 0.0)
-    received = lax.all_to_all(picked, "row", split_axis=2, concat_axis=0, tiled=True)
+    pieces = jnp.split(picked, lax.axis_size("row"), axis=2)
+    incoming = lax.all_to_all(jnp.stack(pieces), "row", 0, 0)
+    received = jnp.concatenate(incoming, axis=0)
     band_rows = jnp.take(received, band_order(first_tile, row_count, rows_each, span_tiles), axis=0)
     band_rows = band_rows.reshape(span_tiles * tile_size, received.shape[2])
     band_rows = lax.fori_loop(0, WINS, left_step, band_rows)

time: 2690 us -> 2550 us (0.948)
  waiting for transfers between devices: 1300 us -> 1120 us
  other arithmetic: 315 us -> 348 us
    all_to_all x1, waiting for transfers between devices: 607 us -> 427 us  [body(): incoming = lax.all_to_all(jnp.stack(pieces), 'row', 0, 0)]
    slice x6 -> x7, local copies, waits for them, and re-layouts: 29.9 us -> 98.8 us  [body(): returned[member]]
    select_n x1 -> x0, local copies, waits for them, and re-layouts: 58.4 us -> none  [body(): jnp.where(row_valid[:, None, None], jnp.take(local_tiles, row_index, axis...]
    unnamed x43 -> x18, local copies, waits for them, and re-layouts: 78.5 us -> 41.7 us
    another operation x0 -> x1, other arithmetic: none -> 34.4 us  [body(): incoming = lax.all_to_all(jnp.stack(pieces), 'row', 0, 0)]
    another operation x0 -> x1, local copies, waits for them, and re-layouts: none -> 32.6 us  [body(): incoming = lax.all_to_all(jnp.stack(pieces), 'row', 0, 0)]
    unnamed x6 -> x1, other arithmetic: 133 us -> 133 us
where the time goes in v1:
time: 2550 us; the launch traced here: 2530 us
  waiting for transfers between devices  1120 us (44%)
  local copies, waits for them, and re-layouts  776 us (30%)
  other arithmetic  348 us (14%)
  matrix products  194 us (8%)
  between operations  33.9 us (1%)
  starting transfers between devices  33.6 us (1%)
  loops' own time  26.1 us (1%)
    all_to_all x1, waiting for transfers between devices, body(): lax.all_to_all(backsend, 'row', split_axis=0, concat_axis=2, tiled=True)  527 us
    all_to_all x1, waiting for transfers between devices, body(): incoming = lax.all_to_all(jnp.stack(pieces), 'row', 0, 0)  427 us
    dynamic_update_slice x10, local copies, waits for them, and re-layouts, left_step(): lax.dynamic_update_slice_in_dim(band_rows, result_rows, offset_row, 0)  222 us
    dot_general x10, matrix products, left_step(): jnp.dot(factor_now.T, window_rows, precision=lax.Precision.HIGHEST, prefe...  174 us
    unnamed x1, other arithmetic  133 us
    all_gather x1, waiting for transfers between devices, body(): all_factors = lax.all_gather(factors, 'col', axis=2, tiled=True)  103 us
    slice x7, local copies, waits for them, and re-layouts, body(): returned[member]  98.8 us
    gather x5, local copies, waits for them, and re-layouts, body(): jnp.take(local_tiles, row_index, axis=0)  76.6 us
  transfers between devices with their start and end apart: 5, of which 5 were waited for; matrix products, arithmetic and copies ran while one was open for 1% of the time, Pallas kernels for 0%

profile of v1, /device:TPU:2, one launch (start us, length us, event | category | flops | bytes accessed | tf_op | source)
XLA Modules:
  0.0 2528.5 jit_solution(3160413552058633533)
XLA Ops:
  9.8 133.4 %reduce.3 = f32[6,128,128,128]{3,2,1,0:T(8,128)} reduce(f32[6,1,128,128,1,128]{5,4,3,2,1,0:T(1,128)} %param.7, f32[]{:T(128)} %broadcast.1276), dimensions={1,4}, to_apply=%param.7.reduce_sub_computation.3 | reduce | bytes 100663296 | tf_op args[0]
  143.1 53.6 %reshape.636 = f32[6,128,16384]{2,1,0:T(8,128)} reshape(f32[6,128,128,128]{3,2,1,0:T(8,128)} %reduce.3) | data formatting | bytes 100663296 | tf_op jit(solution)/shard_map/reshape | solution.py:72
  196.7 22.2 fusion.50
  273.8 34.3 %fusion.10 = f32[6,128,16384]{2,1,0:T(8,128)} fusion(f32[6,128,5376]{2,1,0:T(8,128)} %gather_fusion.7, f32[6,128,5504]{2,1,0:T(8,128)} %gather_fusion.6, f32[6,128,5504]{2,1,0:T(8,128)} %gather_fusion.5, pred[6]{0:T(512)(128)(4,1)S(1)} %get-tuple-element.199, pred[6]{0:T(512)(128)(4,1)S(1)} %get-tuple-element.240), kind=kLoop, calls=%fused_computation.19 | loop fusion | flops 50331648 | bytes 100663312 | tf_op jit(solution)/shard_map/jit(_where)/select_n | solution.py:75
  308.1 32.6 %slice_bitcast_fusion.3 = (f32[1,6,128,4096]{3,2,1,0:T(8,128)}, f32[1,6,128,4096]{3,2,1,0:T(8,128)}, f32[1,6,128,4096]{3,2,1,0:T(8,128)}, f32[1,6,128,4096]{3,2,1,0:T(8,128)}) fusion(f32[6,128,16384]{2,1,0:T(8,128)} %fusion.10), kind=kLoop, calls=%fused_computation.27 | loop fusion | bytes 100663296 | tf_op jit(solution)/shard_map/stack | solution.py:77
  340.7 34.4 %pad_maximum_fusion = f32[4,6,128,4096]{3,2,1,0:T(8,128)} fusion(f32[1,6,128,4096]{3,2,1,0:T(8,128)} %get-tuple-element.212, f32[1,6,128,4096]{3,2,1,0:T(8,128)} %get-tuple-element.213, f32[1,6,128,4096]{3,2,1,0:T(8,128)} %get-tuple-element.214, f32[1,6,128,4096]{3,2,1,0:T(8,128)} %get-tuple-element.211), kind=kLoop, calls=%fused_computation.20 | loop fusion | flops 37748736 | bytes 100663296 | tf_op jit(solution)/shard_map/stack | solution.py:77
  387.8 102.5 %all-gather.2.cloned.1.call-done = f32[10,512,512]{1,2,0:T(8,128)} async-done(((f32[10,512,64]{1,2,0:T(8,128)}), f32[10,512,512]{1,2,0:T(8,128)}) %all-gather.2.cloned.1.call-update) | async-done | bytes 10485776 | tf_op jit(solution)/shard_map/all_gather | solution.py:46
  501.6 427.2 %all-to-all-done = f32[4,6,128,4096]{3,2,1,0:T(8,128)} async-done(((f32[4,6,128,4096]{3,2,1,0:T(8,128)}), f32[4,6,128,4096]{3,2,1,0:T(8,128)}, u32[]{:S(2)}, u32[]{:S(2)}) %all-to-all-start) | async-done | bytes 50331680 | tf_op jit(solution)/shard_map/all_to_all | solution.py:77
  928.8 32.3 %gather_fusion = f32[22,128,4096]{2,1,0:T(8,128)} fusion(f32[24,128,4096]{2,1,0:T(8,128)} %bitcast.12, s32[1024]{0:T(1024)S(1)} %pad_clamp_fusion.4), kind=kCustom, calls=%fused_computation | custom fusion | bytes 92274776 | tf_op jit(solution)/shard_map/jit(_take)/gather | solution.py:79
  961.0 34.3 %bitcast_select_fusion = f32[2816,4096]{1,0:T(8,128)} fusion(f32[22,128,4096]{2,1,0:T(8,128)} %gather_fusion, pred[2816]{0:T(1024)(128)(4,1)S(1)} %broadcast_bitcast_fusion.1), kind=kLoop, calls=%fused_computation.23 | loop fusion | flops 11534336 | bytes 92277504 | tf_op jit(solution)/shard_map/jit(_take)/select_n | solution.py:79
  995.3 414.5 %while.26 = (s32[]{:T(128)}, f32[2816,4096]{1,0:T(8,128)}, f32[10,512,512]{2,1,0:T(8,128)}, s32[10]{0:T(128)S(1)}, s32[]{:T(128)}, /*index=5*/s32[]{:T(128)}, s32[]{:T(128)}) while((s32[]{:T(128)}, f32[2816,4096]{1,0:T(8,128)}, f32[10,512,512]{2,1,0:T(8,128)}, s32[10]{0:T(128)S(1)}, s32[]{:T(128)}, /*index=5*/s32[]{:T(128)}, s32[]{:T(128)}) %tuple.99), condition=%wide.region_1.2_spmd, body=%wide.region_0.1_spmd.sunk | while | flops 12884901888 | bytes 34603672 | solution.py:81
  1014.5 22.2 dynamic_update_slice.27
  1056.0 22.2 dynamic_update_slice.27
  1080.2 17.4 fusion.68
  1097.6 22.2 dynamic_update_slice.27
  1139.1 22.3 dynamic_update_slice.27
  1180.6 22.3 dynamic_update_slice.27
  1222.1 22.3 dynamic_update_slice.27
  1263.6 22.2 dynamic_update_slice.27
  1305.1 22.2 dynamic_update_slice.27
  1346.6 22.3 dynamic_update_slice.27
  1388.2 21.7 dynamic_update_slice.27
  1409.8 35.0 %gather_fusion.1 = f32[24,128,4096]{2,1,0:T(8,128)} fusion(f32[22,128,4096]{2,1,0:T(8,128)} %bitcast.99, s32[1024]{0:T(1024)S(1)} %pad_clamp_fusion.3), kind=kCustom, calls=%fused_computation.1 | custom fusion | bytes 100663392 | tf_op jit(solution)/shard_map/jit(_take)/gather | solution.py:84
  1444.9 35.7 %select_select_fusion = f32[24,128,4096]{2,1,0:T(8,128)} fusion(f32[24,128,4096]{2,1,0:T(8,128)} %gather_fusion.1, pred[24]{0:T(512)(128)(4,1)S(1)} %get-tuple-element.237, pred[24]{0:T(512)(128)(4,1)S(1)} %get-tuple-element.238), kind=kLoop, calls=%fused_computation.22 | loop fusion | flops 25165824 | bytes 100663344 | tf_op jit(solution)/shard_map/jit(_where)/select_n | solution.py:84
  1506.9 527.0 %all-to-all-done.1 = f32[24,128,4096]{2,1,0:T(8,128)} async-done(((f32[24,128,4096]{2,1,0:T(8,128)}), f32[24,128,4096]{2,1,0:T(8,128)}, u32[]{:S(2)}, u32[]{:S(2)}) %all-to-all-start.1) | async-done | bytes 50331680 | tf_op jit(solution)/shard_map/all_to_all | solution.py:85
  2033.9 55.6 %copy.58 = f32[4,6,128,4096]{3,0,2,1:T(4,128)} copy(f32[4,6,128,4096]{3,2,1,0:T(8,128)} %bitcast.17) | data formatting | bytes 100663296 | tf_op jit(solution)/shard_map/all_to_all | solution.py:85
  2089.4 33.1 %fusion.49 = (f32[1,128,4,4096]{3,2,1,0:T(4,128)}, f32[1,128,4,4096]{3,2,1,0:T(4,128)}, f32[1,128,4,4096]{3,2,1,0:T(4,128)}, f32[1,128,4,4096]{3,2,1,0:T(4,128)}...) fusion(f32[6,128,4,4096]{3,2,1,0:T(4,128)} %bitcast.103), kind=kLoop, calls=%fused_computation.183 | loop fusion | bytes 100663296 | tf_op jit(solution)/shard_map/slice | solution.py:89
  2252.2 41.0 %copy.54 = f32[96,8,128,128]{3,2,1,0:T(8,128)} copy(f32[96,8,128,128]{3,1,2,0:T(8,128)} %bitcast.98) | data formatting | bytes 100663296
  2293.2 46.1 %copy.43 = f32[768,128,128]{2,0,1:T(8,128)} copy(f32[768,128,128]{2,1,0:T(8,128)} %bitcast.100) | data formatting | bytes 100663296 | tf_op jit(solution)/shard_map/reshape | solution.py:93
  2349.1 37.6 %all-to-all-done.2 = f32[768,3,128]{2,1,0:T(4,128)S(1)} async-done(((f32[768,3,128]{2,1,0:T(4,128)}), f32[768,3,128]{2,1,0:T(4,128)S(1)}, u32[]{:S(2)}, u32[]{:S(2)}) %all-to-all-start.2) | async-done | bytes 1179680 | tf_op jit(solution)/shard_map/all_to_all | solution.py:98
  2387.5 54.5 %while.27 = (s32[]{:T(128)}, f32[96,2816]{1,0:T(8,128)S(1)}, s32[10]{0:T(128)S(1)}, f32[10,512,512]{2,1,0:T(8,128)}, s32[]{:T(128)}, /*index=5*/s32[]{:T(128)}, s32[]{:T(128)}) while((s32[]{:T(128)}, f32[96,2816]{1,0:T(8,128)S(1)}, s32[10]{0:T(128)S(1)}, f32[10,512,512]{2,1,0:T(8,128)}, s32[]{:T(128)}, /*index=5*/s32[]{:T(128)}, ...), condition=%wide.region_3.4_spmd, body=%wide.region_2.3_spmd.sunk | while | flops 301989888 | bytes 1835671 | solution.py:103
  2454.9 22.0 all-to-all-done.3
  (130 shorter events, 489.4 us)
Async XLA Ops:
  230.7 43.2 %copy-start.2 = (pred[6]{0:T(512)(128)(4,1)}, pred[6]{0:T(512)(128)(4,1)S(1)}, u32[]{:S(2)}) copy-start(pred[6]{0:T(512)(128)(4,1)S(1)} %get-tuple-element.240) | copy-start | bytes 22
  375.1 553.6 %all-to-all-start = ((f32[4,6,128,4096]{3,2,1,0:T(8,128)}), f32[4,6,128,4096]{3,2,1,0:T(8,128)}, u32[]{:S(2)}, u32[]{:S(2)}) async-start(f32[4,6,128,4096]{3,2,1,0:T(8,128)} %pad_maximum_fusion), calls=%async_computation | async-start | bytes 100663296 | tf_op jit(solution)/shard_map/all_to_all | solution.py:77
  386.9 103.5 %all-gather.2.cloned.1.call-start = ((), (), s32[]{:S(2)}) async-start(), calls=%async_computation.4 | async-start | bytes 11796480 | tf_op jit(solution)/shard_map/all_gather | solution.py:46
  961.0 34.3 %copy-start = (s32[10]{0:T(128)S(1)}, s32[10]{0:T(128)}, u32[]{:S(2)}) copy-start(s32[10]{0:T(128)} %param.9) | copy-start | bytes 124
  1480.5 12.5 copy-start.4
  1480.5 25.7 %copy-start.3 = (pred[6]{0:T(512)(128)(4,1)S(1)}, pred[6]{0:T(512)(128)(4,1)}, u32[]{:S(2)}) copy-start(pred[6]{0:T(512)(128)(4,1)} %copy-done.2) | copy-start | bytes 22
  1480.5 553.4 %all-to-all-start.1 = ((f32[24,128,4096]{2,1,0:T(8,128)}), f32[24,128,4096]{2,1,0:T(8,128)}, u32[]{:S(2)}, u32[]{:S(2)}) async-start(f32[24,128,4096]{2,1,0:T(8,128)} %select_select_fusion), calls=%async_computation.1 | async-start | bytes 100663296 | tf_op jit(solution)/shard_map/all_to_all | solution.py:85
  2293.2 48.2 %copy-start.5 = (pred[3]{0:T(512)(128)(4,1)S(1)}, pred[3]{0:T(512)(128)(4,1)}, u32[]{:S(2)}) copy-start(pred[3]{0:T(512)(128)(4,1)} %get-tuple-element.239) | copy-start | bytes 13
  2293.2 48.2 %copy-start.7 = (pred[3]{0:T(512)(128)(4,1)S(1)}, pred[3]{0:T(512)(128)(4,1)}, u32[]{:S(2)}) copy-start(pred[3]{0:T(512)(128)(4,1)} %get-tuple-element.197) | copy-start | bytes 13
  2339.4 48.2 %copy-start.1 = (s32[10]{0:T(128)S(1)}, s32[10]{0:T(128)}, u32[]{:S(2)}) copy-start(s32[10]{0:T(128)} %param.9) | copy-start | bytes 124
  2343.7 43.0 %all-to-all-start.2 = ((f32[768,3,128]{2,1,0:T(4,128)}), f32[768,3,128]{2,1,0:T(4,128)S(1)}, u32[]{:S(2)}, u32[]{:S(2)}) async-start(f32[768,3,128]{2,1,0:T(4,128)} %copy.44), calls=%async_computation.2 | async-start | bytes 3145728 | tf_op jit(solution)/shard_map/all_to_all | solution.py:98
  2386.7 60.9 %copy-start.6 = (s32[3]{0:T(128)S(1)}, s32[3]{0:T(128)}, u32[]{:S(2)}) copy-start(s32[3]{0:T(128)} %get-tuple-element.198) | copy-start | bytes 40
  2444.1 32.9 %all-to-all-start.3 = ((f32[96,24,128]{2,0,1:T(8,128)}), f32[96,24,128]{2,0,1:T(8,128)S(1)}, u32[]{:S(2)}, u32[]{:S(2)}) async-start(f32[96,24,128]{2,0,1:T(8,128)} %select_bitcast_fusion), calls=%async_computation.3 | async-start | bytes 2359296 | tf_op jit(solution)/shard_map/all_to_all | solution.py:110
Sparse Core Ops, SparseCore 0:
  389.3 100.9 all-gather.1
